TPU v7x, 32 devices: a whole 2x2x4 slice. The times are simulated.
32 devices in a mesh: grp: 2 (over y), gx: 4 (over z), gy: 4 (over x, core).
Axes of the slice: x: 2, y: 2, z: 4, core: 2. Of those that a mesh axis runs over, the one named last changes fastest.
Arguments:
- samples: bfloat16 [2816, 65536], P('grp', ('gx', 'gy')), parts along dimension 0, may hold values from -400 to 400
- tile_owner: int32 [256], replicated, may hold values from 0 to 255, each once
Outputs:
- kernel_tiles: float32 [512, 4096], P(('grp', 'gx', 'gy')), parts along dimension 0
There are 2 independent parts, one for each index of `grp`. A program takes and returns all parts, laid end to end along the dimension named above; an argument that names none is the same for every part. Nothing has to cross between parts.
Inputs may be any that keep to these rules, and one draw needn't show every extreme that they name: tile_owner holds each of 0 to 255 once; device k of the group (k = gx index * 4 + gy index) owns slots k * 16 to (k + 1) * 16 - 1; values of 253 and above mark empty slots.
All inputs are finite; a program needn't handle non-finite values.
Results may differ from a plain program's by a relative error of at most 0.0003.
Values sent between devices are 32-bit elements; how exact they have to be, the bound alone decides.
A program may use at most 64 MiB of HBM per device.

v0:
```python
import jax
import jax.numpy as jnp
import numpy as np
from jax import lax
from jax.sharding import PartitionSpec as P

FEATURES = 65536
TILE = 64
NT = 22
NLOW = 253


def tile_coords(order):
    firsts = np.array([k * (k + 1) // 2 for k in range(1, NT)], dtype=np.int32)
    tile_row = jnp.sum((order[:, None] >= jnp.asarray(firsts)[None, :]).astype(jnp.int32), axis=1)
    tile_col = order - tile_row * (tile_row + 1) // 2
    is_live = order < NLOW
    tile_row = jnp.where(is_live, tile_row, 0)
    tile_col = jnp.where(is_live, tile_col, 0)
    return (tile_row, tile_col, is_live)


def shards(samples, tile_owner):
    slots = tile_owner.shape[0] // lax.axis_size(("gx", "gy"))
    stacked = samples.reshape(NT, TILE, samples.shape[1])
    blocked = jnp.einsum("iaf,jbf->ijab", stacked, stacked, preferred_element_type=jnp.float32)
    values = samples.astype(jnp.float32)
    squares = jnp.sum(values * values, axis=1)
    totals = lax.psum(squares, ("gx", "gy"))
    tile_row, tile_col, is_live = tile_coords(tile_owner)
    picked = blocked[tile_row, tile_col].reshape(slots * lax.axis_size(("gx", "gy")), TILE * TILE)
    summed = lax.psum_scatter(
        picked * is_live[:, None].astype(jnp.float32), ("gx", "gy"), scatter_dimension=0, tiled=True
    )
    meansq = totals / FEATURES + 1e-06
    inverse = (1.0 / jnp.sqrt(meansq)).reshape(NT, TILE)
    own_first = lax.axis_index(("gx", "gy")) * slots
    own_order = lax.dynamic_slice_in_dim(tile_owner, own_first, slots)
    tile_row, tile_col, is_live = tile_coords(own_order)
    scaling = (
        inverse[tile_row][:, :, None]
        * inverse[tile_col][:, None, :]
        / jnp.sqrt(jnp.float32(FEATURES))
    )
    return summed * scaling.reshape(slots, TILE * TILE)


def solution(mesh):
    in_specs = (P("grp", ("gx", "gy")), P())
    out_specs = P(("grp", "gx", "gy"), None)
    return jax.shard_map(shards, mesh=mesh, in_specs=in_specs, out_specs=out_specs, check_vma=False)
```

profile of v0, /device:TPU:0, one launch (start us, length us, event | category | flops | bytes accessed | tf_op | source)
XLA Modules:
  0.0 171.4 jit_solution(9900244308594364352)
XLA Ops:
  6.5 0.0 reduce-scatter.4.cloned.1.call-start
  6.5 0.7 compare_convert_fusion
  7.2 0.8 convert_reduce_fusion
  8.0 0.7 fusion.2
  8.7 42.7 %convolution_bitcast_fusion = f32[22,22,64,64]{2,3,0,1:T(8,128)} fusion(bf16[22,64,4096,1]{2,1,3,0:T(8,128)(2,1)} %bitcast.14, bf16[22,64,4096,1]{2,1,0,3:T(8,128)(2,1)} %bitcast.15), kind=kOutput, calls=%fused_computation.4 | convolution fusion | flops 16240345088 | bytes 30998528 | tf_op jit(solution)/shard_map/iaf,jbf->ijab/dot_general | solution.py:26
  51.4 9.9 %gather_fusion = f32[256,64,64]{1,2,0:T(8,128)} fusion(f32[22,22,64,64]{2,3,0,1:T(8,128)} %convolution_bitcast_fusion, s32[256]{0:T(256)S(1)} %fusion.2), kind=kCustom, calls=%fused_computation | custom fusion | bytes 8390656 | tf_op jit(solution)/shard_map/gather | solution.py:31
  61.3 8.6 %copy.13 = f32[256,64,64]{0,2,1:T(8,128)} copy(f32[256,64,64]{1,2,0:T(8,128)} %gather_fusion) | data formatting | bytes 8388608 | tf_op jit(solution)/shard_map/gather | solution.py:31
  69.9 4.4 %bitcast_multiply_fusion = f32[256,4096]{0,1:T(8,128)} fusion(f32[256,64,64]{0,2,1:T(8,128)} %copy.13, f32[256]{0:T(256)S(1)} %compare_convert_fusion), kind=kLoop, calls=%fused_computation.5 | loop fusion | flops 1048576 | bytes 8389632 | tf_op jit(solution)/shard_map/mul | solution.py:33
  74.4 5.6 %copy.18 = f32[256,4096]{1,0:T(8,128)} copy(f32[256,4096]{0,1:T(8,128)} %bitcast_multiply_fusion) | data formatting | bytes 8388608
  80.0 0.0 copy-start
  80.0 0.0 copy-start.1
  80.0 0.0 reduce-scatter.4.cloned.1.call-update
  80.0 6.6 %multiply_reduce_fusion = f32[1408]{0:T(1024)S(1)} fusion(bf16[1408,4096]{1,0:T(8,128)(2,1)} %param.4), kind=kLoop, calls=%fused_computation.3 | loop fusion | flops 17300096 | bytes 11539968 | tf_op jit(solution)/shard_map/reduce_sum | solution.py:28
  86.6 36.2 %psum.7 = f32[1408]{0:T(1024)S(1)} all-reduce(f32[1408]{0:T(1024)S(1)} %multiply_reduce_fusion), channel_id=1, replica_groups=mesh['grp'=2,'gx'=4,'gy'=4] {'gx','gy'}, use_global_device_ids=true, to_apply=%region_3.4 | all-reduce | flops 1408 | bytes 11264 | tf_op jit(solution)/shard_map/psum | solution.py:29
  122.8 0.1 reshape.25
  122.8 0.0 copy-done
  122.8 0.1 dynamic_slice.3
  122.9 0.0 copy-done.1
  122.9 0.2 convert_reduce_fusion.1
  123.1 0.1 compare_select_fusion.3
  123.2 0.6 gather_fusion.2
  123.8 0.1 copy.15
  123.8 0.6 gather_fusion.1
  124.4 0.1 copy.14
  124.5 0.3 multiply_multiply_fusion
  124.8 30.9 %reduce-scatter.4.cloned.1.call-done = f32[16,4096]{1,0:T(8,128)} async-done(((f32[256,4096]{1,0:T(8,128)}), f32[16,4096]{1,0:T(8,128)}) %reduce-scatter.4.cloned.1.call-update) | async-done | bytes 262160
  155.6 2.9 %copy.19 = f32[16,4096]{0,1:T(8,128)} copy(f32[16,4096]{1,0:T(8,128)} %reduce-scatter.4.cloned.1.call-done) | data formatting | bytes 524288
  158.5 3.1 %bitcast_multiply_fusion.1 = f32[16,4096]{0,1:T(8,128)} fusion(f32[16,4096]{0,1:T(8,128)} %copy.19, f32[16,64,64]{0,2,1:T(8,128)S(1)} %multiply_multiply_fusion), kind=kLoop, calls=%fused_computation.6 | loop fusion | flops 65536 | bytes 786432 | tf_op jit(solution)/shard_map/mul | solution.py:45
  161.7 2.9 %copy.16 = f32[16,4096]{1,0:T(8,128)} copy(f32[16,4096]{0,1:T(8,128)} %bitcast_multiply_fusion.1) | data formatting | bytes 524288 | tf_op jit(solution)/shard_map/mul | solution.py:45
  (2 shorter events, 0.0 us)
Async XLA Ops:
  6.5 149.1 %reduce-scatter.4.cloned.1.call-start = ((), (), s32[]{:S(2)}) async-start(), calls=%async_computation.1 | async-start | bytes 4456448
  80.0 42.8 %copy-start = (s32[256]{0:T(256)S(1)}, s32[256]{0:T(256)}, u32[]{:S(2)}) copy-start(s32[256]{0:T(256)} %param.5) | copy-start | bytes 3076
  80.0 42.9 %copy-start.1 = (s32[21]{0:T(128)S(1)}, s32[21]{0:T(128)}, u32[]{:S(2)}) copy-start(s32[21]{0:T(128)} %constant.60.clone) | copy-start | bytes 256
Sparse Core Ops, SparseCore 0:
  80.1 75.4 reduce-scatter.3
where the time goes:
time: 172 us; the launch traced here: 171 us
  matrix products  42.7 us (25%)
  blocking collectives  36.2 us (21%)
  local copies, waits for them, and re-layouts  31.4 us (18%)
  waiting for transfers between devices  30.9 us (18%)
  other arithmetic  16.8 us (10%)
  between operations  13.4 us (8%)
    dot_general x1, matrix products, shards(): jnp.einsum('iaf,jbf->ijab', stacked, stacked, preferred_element_type=jnp....  42.7 us
    psum x1, blocking collectives, shards(): totals = lax.psum(squares, ('gx', 'gy'))  36.2 us
    unnamed x2, waiting for transfers between devices  30.9 us
    gather x2, local copies, waits for them, and re-layouts, shards(): blocked[tile_row, tile_col]  18.6 us
    unnamed x6, local copies, waits for them, and re-layouts  8.53 us
    reduce_sum x1, other arithmetic, shards(): squares = jnp.sum(values * values, axis=1)  6.57 us
    mul x1, other arithmetic, shards(): picked * is_live[:, None].astype(jnp.float32)  4.43 us
  transfers between devices with their start and end apart: 1, of which 1 were waited for; matrix products, arithmetic and copies ran while one was open for 5% of the time, Pallas kernels for 0%

commit v1 on v0

v1 whole, which is shorter than its diff:
```python
import functools

import jax
import jax.numpy as jnp
import numpy as np
from jax import lax
from jax.experimental import pallas as pl
from jax.experimental.pallas import tpu as pltpu
from jax.sharding import PartitionSpec as P

TILE = 64
HALF = TILE // 2
QUART = TILE // 4
ROWS = 256
MESH = pl.DeviceIdType.MESH


def tri(k):
    return k * (k + 1) // 2


def tables(slots_all, nt):
    dead = 8 * tri(nt // 2)
    table = np.zeros((6, slots_all), np.int32)
    table[0], table[1] = dead, dead
    t = 0
    for i in range(nt):
        for j in range(i + 1):
            first = 4 * (2 * (tri(i // 2) + j // 2) + i % 2)
            side = j % 2
            table[:, t] = (first + 2 * side, first + 2 * (1 - side), side, i, j // 2, side)
            t += 1
    assert t <= slots_all
    return table


def kernel(cfg, owner_ref, table_ref, x_ref, out_ref, a, g, h, buf, dg, inv, colb, scale, pk, flat,
           load_sem, pair_send, pair_recv, diag_send, diag_recv, ring_send, ring_recv):
    gx_n, gy_n, slots, nsub, features = cfg
    ring_n = gx_n * gy_n // 2
    sub = slots // nsub
    ns = a.shape[0]
    np_ = ns // 128
    gx, gy = lax.axis_index("gx"), lax.axis_index("gy")
    core = gy % 2
    row = gy // 2
    pos = row * gx_n + jnp.where(row % 2 == 0, gx, gx_n - 1 - gx)

    def coords_of(p):
        r = p // gx_n
        c = p % gx_n
        c = jnp.where(r % 2 == 0, c, gx_n - 1 - c)
        return c, r * 2 + core

    def device_of(p):
        c, y = coords_of(p)
        return {"gx": c, "gy": y}

    def first_slot(p):
        c, y = coords_of(p)
        return (c * gy_n + y) * slots

    partner = {"gx": gx, "gy": gy + 1 - 2 * core}

    starts = list(range(0, ns, ROWS))
    loads = []
    for n, r0 in enumerate(starts):
        size = min(ROWS, ns - r0)
        loads.append(pltpu.make_async_copy(x_ref.at[pl.ds(r0, size)], a.at[pl.ds(r0, size)], load_sem.at[n]))
        loads[-1].start()

    barrier = pltpu.get_barrier_semaphore()
    pl.semaphore_signal(barrier, inc=1, device_id=partner, device_id_type=MESH)

    @pl.loop(1, ring_n)
    def _(o):
        pl.semaphore_signal(barrier, inc=1, device_id=device_of((pos + o) % ring_n), device_id_type=MESH)

    dead = 8 * tri(np_)
    for n in range(4):
        g[dead + n] = jnp.zeros((QUART, 128), jnp.float32)
        h[dead + n] = jnp.zeros((QUART, 128), jnp.float32)

    def product(r0, size, c0, width):
        return lax.dot_general(
            a[pl.ds(r0, size), :], a[pl.ds(c0, width), :],
            (((1,), (1,)), ((), ())), preferred_element_type=jnp.float32,
        )

    def put(block, value):
        g[pl.ds(8 * block, 8)] = value.reshape(8, QUART, 128)

    pair_copies = []
    for n, r0 in enumerate(starts):
        size = min(ROWS, ns - r0)
        nq = size // 128
        loads[n].wait()

        if n:
            @pl.loop(0, n)
            def _(j):
                value = product(r0, size, pl.multiple_of(j * ROWS, ROWS), ROWS)
                for u in range(nq):
                    for v in range(2):
                        put(tri(r0 // 128 + u) + 2 * j + v, value[u * 128:(u + 1) * 128, v * 128:(v + 1) * 128])

        value = product(r0, size, r0, size)
        for u in range(nq):
            for v in range(u + 1):
                put(tri(r0 // 128 + u) + 2 * n + v, value[u * 128:(u + 1) * 128, v * 128:(v + 1) * 128])
        if n == 0:
            pl.semaphore_wait(barrier, ring_n)
        first, last = 8 * tri(r0 // 128), 8 * tri(r0 // 128 + nq)
        copy = pltpu.make_async_remote_copy(
            src_ref=g.at[pl.ds(first, last - first)], dst_ref=h.at[pl.ds(first, last - first)],
            send_sem=pair_send.at[n], recv_sem=pair_recv.at[n], device_id=partner, device_id_type=MESH)
        copy.start()
        pair_copies.append(copy)
    for copy in pair_copies:
        copy.wait_recv()

    lane_half = lax.broadcasted_iota(jnp.int32, (QUART, 128), 1) // TILE

    def picked(slot, d):
        tile = owner_ref[slot]
        near = table_ref[0, tile] + d
        far = table_ref[1, tile] + d
        z = g[near] + h[near]
        y = g[far] + h[far]
        return jnp.where(lane_half == table_ref[2, tile], z, pltpu.roll(y, TILE, 1))

    def ring_copy(d, step, s):
        src = buf.at[d, step, pl.ds(s * sub, sub)]
        dst = buf.at[d, step + 1, pl.ds(s * sub, sub)]
        target = device_of((pos + (1 if d == 0 else ring_n - 1)) % ring_n)
        return pltpu.make_async_remote_copy(
            src_ref=src, dst_ref=dst, send_sem=ring_send.at[d, step, s], recv_sem=ring_recv.at[d, step, s],
            device_id=target, device_id_type=MESH)

    def chunk_of(d, step):
        if d == 0:
            return (pos + 2 * ring_n - 1 - step) % ring_n
        return (pos + 1 + step) % ring_n

    base = [first_slot(chunk_of(d, 0)) for d in range(2)]

    @pl.loop(0, nsub)
    def _(s):
        for d in range(2):
            for k in range(sub):
                buf[d, 0, s * sub + k] = picked(base[d] + s * sub + k, d)
            ring_copy(d, 0, s).start()

    eye = (lax.broadcasted_iota(jnp.int32, (128, 128), 0) == lax.broadcasted_iota(jnp.int32, (128, 128), 1))
    for p in range(np_):
        block = tri(p) + p
        whole = (g[pl.ds(8 * block, 8)] + h[pl.ds(8 * block, 8)]).reshape(128, 128)
        both = jnp.where(eye, whole, 0.0)
        dg[pos, pl.ds(p, 1), :] = jnp.sum(both, axis=0, keepdims=True)

    def diag_copy(o):
        return pltpu.make_async_remote_copy(
            src_ref=dg.at[pos], dst_ref=dg.at[pos], send_sem=diag_send.at[o], recv_sem=diag_recv.at[o],
            device_id=device_of((pos + o) % ring_n), device_id_type=MESH)

    @pl.loop(1, ring_n)
    def _(o):
        diag_copy(o).start()

    def ring_step(step):
        first = [first_slot(chunk_of(d, step)) for d in range(2)]

        @pl.loop(0, nsub)
        def _(s):
            for d in range(2):
                ring_copy(d, step - 1, s).wait_recv()
                for k in range(sub):
                    buf[d, step, s * sub + k] += picked(first[d] + s * sub + k, d)
                ring_copy(d, step, s).start()

    split = min(3, ring_n - 1)

    @pl.loop(1, split)
    def _(step):
        ring_step(step)

    @pl.loop(1, ring_n)
    def _(o):
        diag_copy(o).wait_recv()

    total = dg[0]
    total = lax.fori_loop(1, ring_n, lambda r, acc: acc + dg[r], total)
    inverse = 1.0 / jnp.sqrt(total / features + 1e-06)
    for p in range(np_):
        line = inverse[p:p + 1, :]
        inv[p] = jnp.broadcast_to(line, (8, 128))
        across = jnp.broadcast_to(line, (128, 128)).T
        colb[2 * p] = across[:TILE]
        colb[2 * p + 1] = across[TILE:]

    own = (gx * gy_n + gy) * slots
    wide_half = lax.broadcasted_iota(jnp.int32, (HALF, 128), 1) // TILE
    one_half = lax.broadcasted_iota(jnp.int32, (8, 128), 1) // TILE
    root = 1.0 / jnp.sqrt(jnp.float32(features))

    @pl.loop(0, slots)
    def _(k):
        tile = owner_ref[own + k]
        down = colb[table_ref[3, tile]]
        down = jnp.where(wide_half == 0, down[:HALF], down[HALF:])
        line = inv[table_ref[4, tile]]
        line = jnp.where(one_half == table_ref[5, tile], line, pltpu.roll(line, TILE, 1))
        scale[k] = down * line[:1] * root

    @pl.loop(split, ring_n - 1)
    def _(step):
        ring_step(step)

    left = lax.broadcasted_iota(jnp.int32, (8, 128), 1) < TILE

    @pl.loop(0, nsub)
    def _(s):
        for d in range(2):
            ring_copy(d, ring_n - 2, s).wait_recv()
            for k in range(sub):
                n = s * sub + k
                value = buf[d, ring_n - 1, n] + picked(own + n, d)
                spot = (2 * k + d) * QUART
                pk[pl.ds(spot, QUART), :] = value * scale[n, d * QUART:(d + 1) * QUART, :]
                even = pk[pl.ds(spot, 8, stride=2), :]
                odd = pk[pl.ds(spot + 1, 8, stride=2), :]
                flat[pl.ds(pl.multiple_of(n * HALF + d * 8, 8), 8), :] = jnp.where(left, even, pltpu.roll(odd, TILE, 1))
                flat[pl.ds(pl.multiple_of(n * HALF + QUART + d * 8, 8), 8), :] = jnp.where(left, pltpu.roll(even, TILE, 1), odd)

    for r in range(HALF):
        out_ref[:, r * 128:(r + 1) * 128] = flat[pl.ds(r, slots, stride=HALF), :]

    for copy in pair_copies:
        copy.wait_send()

    @pl.loop(1, ring_n)
    def _(o):
        diag_copy(o).wait_send()

    @pl.loop(0, ring_n - 1)
    def _(step):
        @pl.loop(0, nsub)
        def _(s):
            for d in range(2):
                ring_copy(d, step, s).wait_send()


def shards(gx_n, gy_n, samples, tile_owner):
    ns, depth = samples.shape
    slots = tile_owner.shape[0] // (gx_n * gy_n)
    nsub = 4 if slots % 4 == 0 else 1
    ring_n = gx_n * gy_n // 2
    np_ = ns // 128
    blocks = 8 * tri(np_) + 4
    nload = -(-ns // ROWS)
    nlines = -(-np_ // 8) * 8
    cfg = (gx_n, gy_n, slots, nsub, depth * gx_n * gy_n)
    f32 = jnp.float32
    dma = pltpu.SemaphoreType.DMA
    table = jnp.asarray(tables(tile_owner.shape[0], ns // TILE))
    smem = pl.BlockSpec(memory_space=pltpu.SMEM)
    return pl.pallas_call(
        functools.partial(kernel, cfg),
        out_shape=jax.ShapeDtypeStruct((slots, TILE * TILE), f32),
        in_specs=[smem, smem, pl.BlockSpec(memory_space=pl.ANY)],
        out_specs=pl.BlockSpec(memory_space=pltpu.VMEM),
        scratch_shapes=[
            pltpu.VMEM((ns, depth), samples.dtype),
            pltpu.VMEM((blocks, QUART, 128), f32),
            pltpu.VMEM((blocks, QUART, 128), f32),
            pltpu.VMEM((2, ring_n, slots, QUART, 128), f32),
            pltpu.VMEM((ring_n, nlines, 128), f32),
            pltpu.VMEM((np_, 8, 128), f32),
            pltpu.VMEM((2 * np_, TILE, 128), f32),
            pltpu.VMEM((slots, HALF, 128), f32),
            pltpu.VMEM((2 * (slots // nsub) * QUART, 128), f32),
            pltpu.VMEM((slots * HALF, 128), f32),
            dma((nload,)), dma((nload,)), dma((nload,)),
            dma((ring_n,)), dma((ring_n,)),
            dma((2, ring_n - 1, nsub)), dma((2, ring_n - 1, nsub)),
        ],
        compiler_params=pltpu.CompilerParams(
            collective_id=0, has_side_effects=True, vmem_limit_bytes=56 * 1024 * 1024
        ),
    )(tile_owner, table, samples)


def solution(mesh):
    in_specs = (P("grp", ("gx", "gy")), P())
    out_specs = P(("grp", "gx", "gy"), None)
    body = functools.partial(shards, mesh.shape["gx"], mesh.shape["gy"])
    return jax.shard_map(body, mesh=mesh, in_specs=in_specs, out_specs=out_specs, check_vma=False)
```

time: 172 us -> 53.2 us (0.31)
  Pallas kernels: 0 us -> 51.3 us
  matrix products: 42.7 us -> 0 us
  blocking collectives: 36.2 us -> 0 us
  waiting for transfers between devices: 30.9 us -> 0 us
  local copies, waits for them, and re-layouts: 31.4 us -> 1.67 us
  other arithmetic: 16.8 us -> 0 us
  between operations: 13.4 us -> 0.01 us
    pallas_call x0 -> x1, Pallas kernels: none -> 51.3 us  [shards(): pl.pallas_call(functools.partial(kernel, cfg), out_shape=jax.ShapeDtypeSt...]
    dot_general x1 -> x0, matrix products: 42.7 us -> none  [shards(): jnp.einsum('iaf,jbf->ijab', stacked, stacked, preferred_element_type=jnp....]
    psum x1 -> x0, blocking collectives: 36.2 us -> none  [shards(): totals = lax.psum(squares, ('gx', 'gy'))]
    unnamed x2 -> x0, waiting for transfers between devices: 30.9 us -> none
    gather x6 -> x0, local copies, waits for them, and re-layouts: 19.8 us -> none  [the longest x2 18.6 us: shards(): blocked[tile_row, tile_col]]
    mul x2 -> x0, other arithmetic: 7.57 us -> none  [the longest x1 4.43 us: shards(): picked * is_live[:, None].astype(jnp.float32)]
    reduce_sum x3 -> x0, other arithmetic: 7.52 us -> none  [the longest x1 6.57 us: shards(): squares = jnp.sum(values * values, axis=1)]
    unnamed x6 -> x1, local copies, waits for them, and re-layouts: 8.53 us -> 1.67 us
  transfers between devices with their start and end apart: 1 -> 0, of which waited for: 1 -> 0; matrix products, arithmetic and copies ran while one was open for 5% -> 0% of each run, Pallas kernels for 0% -> 0%
where the time goes in v1:
time: 53.2 us; the launch traced here: 52.9 us
  Pallas kernels  51.3 us (96%)
  local copies, waits for them, and re-layouts  1.67 us (3%)
    pallas_call x1, Pallas kernels, shards(): pl.pallas_call(functools.partial(kernel, cfg), out_shape=jax.ShapeDtypeSt...  51.3 us
    unnamed x1, local copies, waits for them, and re-layouts  1.67 us

profile of v1, /device:TPU:0, one launch (start us, length us, event | category | flops | bytes accessed | tf_op | source)
XLA Modules:
  0.0 52.9 jit_solution(616299297447362665)
XLA Ops:
  0.0 51.3 %shard_map.37 = f32[16,4096]{1,0:T(8,128)} custom-call(s32[256]{0:T(256)} %owner_ref.1, s32[6,256]{1,0:T(8,128)} %constant.2.clone.table_ref, bf16[1408,4096]{1,0:T(8,128)(2,1)} %x_ref.1), custom_call_target="tpu_custom_call" | custom-call | tf_op jit(solution)/shard_map/pallas_call | solution.py:267
  51.3 1.7 %copy.5 = f32[16,4096]{1,0:T(8,128)} copy(f32[16,4096]{1,0:T(8,128)} %shard_map.37) | data formatting | bytes 524288

commit v2 on v1

--- a/solution.py
+++ b/solution.py
@@ -11,7 +11,7 @@
 TILE = 64
 HALF = TILE // 2
 QUART = TILE // 4
-ROWS = 256
+ROWS = 512
 MESH = pl.DeviceIdType.MESH
 
 
@@ -19,14 +19,25 @@
     return k * (k + 1) // 2
 
 
-def tables(slots_all, nt):
-    dead = 8 * tri(nt // 2)
+def spots(ns):
+    spot = {}
+    for r0 in range(0, ns, ROWS):
+        rows = range(r0 // 128, min(r0 + ROWS, ns) // 128)
+        for c0 in range(0, r0 + 1, ROWS):
+            for q in rows:
+                for p in range(c0 // 128, min(q + 1, (c0 + ROWS) // 128)):
+                    spot[q, p] = len(spot)
+    return spot
+
+
+def tables(slots_all, ns):
+    spot = spots(ns)
     table = np.zeros((6, slots_all), np.int32)
-    table[0], table[1] = dead, dead
+    table[0], table[1] = 8 * len(spot), 8 * len(spot)
     t = 0
-    for i in range(nt):
+    for i in range(ns // TILE):
         for j in range(i + 1):
-            first = 4 * (2 * (tri(i // 2) + j // 2) + i % 2)
+            first = 4 * (2 * spot[i // 2, j // 2] + i % 2)
             side = j % 2
             table[:, t] = (first + 2 * side, first + 2 * (1 - side), side, i, j // 2, side)
             t += 1
@@ -90,10 +101,22 @@
     def put(block, value):
         g[pl.ds(8 * block, 8)] = value.reshape(8, QUART, 128)
 
+    spot = spots(ns)
+    per = ROWS // 128
     pair_copies = []
+    started = 0
+
+    def pair_copy(first, last):
+        many = pl.ds(8 * first, 8 * (last - first))
+        n = len(pair_copies)
+        pair_copies.append(pltpu.make_async_remote_copy(
+            src_ref=g.at[many], dst_ref=h.at[many], send_sem=pair_send.at[n], recv_sem=pair_recv.at[n],
+            device_id=partner, device_id_type=MESH))
+
     for n, r0 in enumerate(starts):
         size = min(ROWS, ns - r0)
         nq = size // 128
+        q0 = r0 // 128
         loads[n].wait()
 
         if n:
@@ -101,21 +124,25 @@
             def _(j):
                 value = product(r0, size, pl.multiple_of(j * ROWS, ROWS), ROWS)
                 for u in range(nq):
-                    for v in range(2):
-                        put(tri(r0 // 128 + u) + 2 * j + v, value[u * 128:(u + 1) * 128, v * 128:(v + 1) * 128])
+                    for v in range(per):
+                        put(spot[q0, 0] + j * nq * per + u * per + v,
+                            value[u * 128:(u + 1) * 128, v * 128:(v + 1) * 128])
+
+            pair_copy(spot[q0, 0], spot[q0, q0])
+            if not started:
+                pl.semaphore_wait(barrier, ring_n)
+            for copy in pair_copies[started:]:
+                copy.start()
+            started = len(pair_copies)
 
         value = product(r0, size, r0, size)
         for u in range(nq):
             for v in range(u + 1):
-                put(tri(r0 // 128 + u) + 2 * n + v, value[u * 128:(u + 1) * 128, v * 128:(v + 1) * 128])
-        if n == 0:
-            pl.semaphore_wait(barrier, ring_n)
-        first, last = 8 * tri(r0 // 128), 8 * tri(r0 // 128 + nq)
-        copy = pltpu.make_async_remote_copy(
-            src_ref=g.at[pl.ds(first, last - first)], dst_ref=h.at[pl.ds(first, last - first)],
-            send_sem=pair_send.at[n], recv_sem=pair_recv.at[n], device_id=partner, device_id_type=MESH)
-        copy.start()
-        pair_copies.append(copy)
+                put(spot[q0 + u, q0 + v], value[u * 128:(u + 1) * 128, v * 128:(v + 1) * 128])
+        pair_copy(spot[q0, q0], spot[q0 + nq - 1, q0 + nq - 1] + 1)
+        if started:
+            pair_copies[-1].start()
+            started += 1
     for copy in pair_copies:
         copy.wait_recv()
 
@@ -153,7 +180,7 @@
 
     eye = (lax.broadcasted_iota(jnp.int32, (128, 128), 0) == lax.broadcasted_iota(jnp.int32, (128, 128), 1))
     for p in range(np_):
-        block = tri(p) + p
+        block = spot[p, p]
         whole = (g[pl.ds(8 * block, 8)] + h[pl.ds(8 * block, 8)]).reshape(128, 128)
         both = jnp.where(eye, whole, 0.0)
         dg[pos, pl.ds(p, 1), :] = jnp.sum(both, axis=0, keepdims=True)
@@ -262,7 +289,7 @@
     cfg = (gx_n, gy_n, slots, nsub, depth * gx_n * gy_n)
     f32 = jnp.float32
     dma = pltpu.SemaphoreType.DMA
-    table = jnp.asarray(tables(tile_owner.shape[0], ns // TILE))
+    table = jnp.asarray(tables(tile_owner.shape[0], ns))
     smem = pl.BlockSpec(memory_space=pltpu.SMEM)
     return pl.pallas_call(
         functools.partial(kernel, cfg),
@@ -280,7 +307,7 @@
             pltpu.VMEM((slots, HALF, 128), f32),
             pltpu.VMEM((2 * (slots // nsub) * QUART, 128), f32),
             pltpu.VMEM((slots * HALF, 128), f32),
-            dma((nload,)), dma((nload,)), dma((nload,)),
+            dma((nload,)), dma((2 * nload - 1,)), dma((2 * nload - 1,)),
             dma((ring_n,)), dma((ring_n,)),
             dma((2, ring_n - 1, nsub)), dma((2, ring_n - 1, nsub)),
         ],

time: 53.2 us -> 50.9 us (0.957)
  Pallas kernels: 51.3 us -> 49 us
    pallas_call x1, Pallas kernels: 51.3 us -> 49 us  [shards(): pl.pallas_call(functools.partial(kernel, cfg), out_shape=jax.ShapeDtypeSt...]
where the time goes in v2:
time: 50.9 us; the launch traced here: 50.7 us
  Pallas kernels  49 us (96%)
  local copies, waits for them, and re-layouts  1.67 us (3%)
    pallas_call x1, Pallas kernels, shards(): pl.pallas_call(functools.partial(kernel, cfg), out_shape=jax.ShapeDtypeSt...  49 us
    unnamed x1, local copies, waits for them, and re-layouts  1.67 us

profile of v2, /device:TPU:0, one launch (start us, length us, event | category | flops | bytes accessed | tf_op | source)
XLA Modules:
  0.0 50.7 jit_solution(4706179944914306570)
XLA Ops:
  0.0 49.0 %shard_map.37 = f32[16,4096]{1,0:T(8,128)} custom-call(s32[256]{0:T(256)} %owner_ref.1, s32[6,256]{1,0:T(8,128)} %constant.2.clone.table_ref, bf16[1408,4096]{1,0:T(8,128)(2,1)} %x_ref.1), custom_call_target="tpu_custom_call" | custom-call | tf_op jit(solution)/shard_map/pallas_call | solution.py:294
  49.0 1.7 %copy.5 = f32[16,4096]{1,0:T(8,128)} copy(f32[16,4096]{1,0:T(8,128)} %shard_map.37) | data formatting | bytes 524288

commit v3 on v2

--- a/solution.py
+++ b/solution.py
@@ -285,7 +285,6 @@
     np_ = ns // 128
     blocks = 8 * tri(np_) + 4
     nload = -(-ns // ROWS)
-    nlines = -(-np_ // 8) * 8
     cfg = (gx_n, gy_n, slots, nsub, depth * gx_n * gy_n)
     f32 = jnp.float32
     dma = pltpu.SemaphoreType.DMA
@@ -301,12 +300,12 @@
             pltpu.VMEM((blocks, QUART, 128), f32),
             pltpu.VMEM((blocks, QUART, 128), f32),
             pltpu.VMEM((2, ring_n, slots, QUART, 128), f32),
-            pltpu.VMEM((ring_n, nlines, 128), f32),
+            pltpu.VMEM((ring_n, np_, 128), f32),
             pltpu.VMEM((np_, 8, 128), f32),
             pltpu.VMEM((2 * np_, TILE, 128), f32),
             pltpu.VMEM((slots, HALF, 128), f32),
-            pltpu.VMEM((2 * (slots // nsub) * QUART, 128), f32),
-            pltpu.VMEM((slots * HALF, 128), f32),
+            pltpu.VMEM((2 * (slots // nsub) * QUART + 8, 128), f32),
+            pltpu.VMEM(((slots + 1) * HALF, 128), f32),
             dma((nload,)), dma((2 * nload - 1,)), dma((2 * nload - 1,)),
             dma((ring_n,)), dma((ring_n,)),
             dma((2, ring_n - 1, nsub)), dma((2, ring_n - 1, nsub)),

time: 50.9 us -> 50.6 us (level)
  no operation moved by 1% of the time
where the time goes in v3:
time: 50.6 us; the launch traced here: 50.4 us
  Pallas kernels  48.7 us (96%)
  local copies, waits for them, and re-layouts  1.67 us (3%)
    pallas_call x1, Pallas kernels, shards(): pl.pallas_call(functools.partial(kernel, cfg), out_shape=jax.ShapeDtypeSt...  48.7 us
    unnamed x1, local copies, waits for them, and re-layouts  1.67 us

profile of v3, /device:TPU:0, one launch (start us, length us, event | category | flops | bytes accessed | tf_op | source)
XLA Modules:
  0.0 50.4 jit_solution(1994258606269392913)
XLA Ops:
  0.0 48.7 %shard_map.37 = f32[16,4096]{1,0:T(8,128)} custom-call(s32[256]{0:T(256)} %owner_ref.1, s32[6,256]{1,0:T(8,128)} %constant.2.clone.table_ref, bf16[1408,4096]{1,0:T(8,128)(2,1)} %x_ref.1), custom_call_target="tpu_custom_call" | custom-call | tf_op jit(solution)/shard_map/pallas_call | solution.py:293
  48.7 1.7 %copy.5 = f32[16,4096]{1,0:T(8,128)} copy(f32[16,4096]{1,0:T(8,128)} %shard_map.37) | data formatting | bytes 524288
